TPU v7x, 256 devices: a whole 4x4x8 slice. The times are simulated.
256 devices in a mesh: stn: 32 (over z, x_lo, core), tm: 8 (over x_hi, y).
Axes of the slice: x: 4 (x_hi: 2, x_lo: 2; x = x_hi * 2 + x_lo), y: 4, z: 8, core: 2. Of those that a mesh axis runs over, the one named last changes fastest.
Arguments:
- voltage: bfloat16 [256, 256, 2, 4096], P('stn', 'tm'), may hold values from -6 to 6
- fir_taps: float32 [16, 4096], replicated, may hold values from -1.5 to 1.5
Outputs:
- visibilities: float32 [2, 256, 32, 2048], P(None, 'stn', None, 'tm')
All inputs are finite; a program needn't handle non-finite values.
Results may differ from a plain program's by a relative error of at most 0.0014.
Values may be sent and summed in bfloat16 or wider, within the bound.
A program may use at most 192 MiB of HBM per device.

v0:
```python
import math

import jax
import jax.numpy as jnp
from jax import lax
from jax.sharding import PartitionSpec as P

NCH = 4096
ROOT = 64
CHANS = 2048
VISITS = 4


def passed_along(block, axis, distance):
    devices = range(lax.axis_size(axis))
    route = [((i - distance) % len(devices), i) for i in devices]
    return lax.ppermute(block, axis, route)


def passed_along_2(shard, axis, by):
    peers = lax.axis_size(axis)
    pairs = [(i, i + by) for i in range(peers) if 0 <= i + by < peers]
    return lax.ppermute(shard, axis, pairs)


def tables(size_a, size_b, modulus, factor):
    left_index = lax.iota(jnp.int32, size_a)[:, None]
    right_index = lax.iota(jnp.int32, size_b)[None, :]
    angles = (left_index * right_index % modulus).astype(jnp.float32) * (2.0 * math.pi / modulus)
    return (jnp.cos(angles) * factor, jnp.sin(angles) * factor)


def real_form(cosine, sine_part):
    from_real = jnp.stack([cosine, -sine_part], axis=1)
    from_imag = jnp.stack([sine_part, cosine], axis=1)
    return jnp.stack([from_real, from_imag], axis=0)


def channelise(voltage, history, fir_taps):
    count_frames = voltage.shape[1]
    signals = voltage.shape[0]
    width_all = 2 * voltage.shape[3]
    extended = jnp.concatenate([history, voltage], 1)
    extended = extended.reshape(signals, extended.shape[1], width_all).astype(jnp.float32)
    kernel = jnp.tile(fir_taps, (1, 2))[:, None, :]
    filtered = lax.conv_general_dilated(
        extended,
        kernel,
        (1,),
        "VALID",
        dimension_numbers=("NHC", "HIO", "NHC"),
        feature_group_count=width_all,
        precision=lax.Precision.HIGHEST,
    )
    grid_form = filtered.reshape(signals, count_frames, 2, ROOT, ROOT)
    cos_one, sin_one = tables(ROOT, ROOT, ROOT, 1.0)
    section_one = jnp.einsum(
        "sfrab,rapk->sfbpk", grid_form, real_form(cos_one, sin_one), precision=lax.Precision.HIGHEST
    )
    cos_turn, sin_turn = tables(ROOT, ROOT, NCH, 1.0)
    real_part = section_one[:, :, :, 0]
    imag_part = section_one[:, :, :, 1]
    turned = jnp.stack(
        [real_part * cos_turn + imag_part * sin_turn, imag_part * cos_turn - real_part * sin_turn],
        3,
    )
    keep_count = CHANS // ROOT
    cos_two, sin_two = tables(ROOT, keep_count, ROOT, 1.0 / math.sqrt(NCH))
    spectrum = jnp.einsum(
        "sfbpk,pbqj->sfqjk", turned, real_form(cos_two, sin_two), precision=lax.Precision.HIGHEST
    )
    return spectrum.reshape(signals, count_frames, 2, CHANS).astype(jnp.bfloat16)


def correlate(own_block, other_block):
    products = jnp.einsum(
        "sfrc,tfqc->rsqtc", own_block, other_block, preferred_element_type=jnp.float32
    )
    real_part = products[0, :, 0] + products[1, :, 1]
    imag_part = products[1, :, 0] - products[0, :, 1]
    return jnp.stack([real_part, imag_part], 0)


def partner_blocks(local_block):
    blocks = [local_block]
    current = local_block
    for visit_index in range(1, VISITS):
        current = passed_along(current, "stn", 1)
        blocks.append(current)
    return blocks


def local(voltage, fir_taps):
    frames_here = voltage.shape[1]
    tail_frames = voltage[:, frames_here - (fir_taps.shape[0] - 1) :]
    history = passed_along_2(tail_frames, "tm", 1)
    spectrum = channelise(voltage, history, fir_taps)
    local_block = lax.all_to_all(spectrum, "tm", split_axis=3, concat_axis=1, tiled=True)
    blocks = partner_blocks(local_block)
    partial_value = jnp.concatenate(
        [correlate(local_block, visiting_block) for visiting_block in blocks], 2
    )
    return partial_value / float(lax.axis_size("tm") * frames_here)


def solution(mesh):
    return jax.shard_map(
        local,
        mesh=mesh,
        in_specs=(P("stn", "tm", None, None), P()),
        out_specs=P(None, "stn", None, "tm"),
        check_vma=False,
    )
```

profile of v0, /device:TPU:99, one launch (start us, length us, event | category | flops | bytes accessed | tf_op | source)
XLA Modules:
  0.0 348.3 jit_solution(5081609641618378158)
XLA Ops:
  0.0 5.3 %slice.57 = bf16[8,15,2,4096]{3,2,1,0:T(2,128)(2,1)} slice(bf16[8,32,2,4096]{3,2,1,0:T(2,128)(2,1)} %param.2), slice={[0:8], [17:32], [0:2], [0:4096]} | slice | bytes 3932160 | tf_op jit(solution)/shard_map/slice | solution.py:95
  11.3 39.0 %collective-permute-done = bf16[8,15,2,4096]{3,2,1,0:T(2,128)(2,1)S(1)} collective-permute-done((bf16[8,15,2,4096]{3,2,1,0:T(2,128)(2,1)}, bf16[8,15,2,4096]{3,2,1,0:T(2,128)(2,1)S(1)}, u32[]{:S(2)}, u32[]{:S(2)}) %collective-permute-start) | collective-permute-done | bytes 1966112 | tf_op jit(solution)/shard_map/ppermute | solution.py:23
  50.3 18.0 %pad_maximum_fusion = bf16[8,47,2,4096]{3,2,1,0:T(2,128)(2,1)S(1)} fusion(bf16[8,32,2,4096]{3,2,1,0:T(2,128)(2,1)} %param.2, bf16[8,15,2,4096]{3,2,1,0:T(2,128)(2,1)S(1)} %collective-permute-done), kind=kLoop, calls=%fused_computation.10 | loop fusion | flops 3080192 | bytes 12320768 | tf_op jit(solution)/shard_map/concatenate | solution.py:43
  68.3 7.0 %copy.49 = bf16[8,47,2,4096]{3,0,2,1:T(8,128)(2,1)S(1)} copy(bf16[8,47,2,4096]{3,2,1,0:T(2,128)(2,1)S(1)} %pad_maximum_fusion) | data formatting | bytes 12320768 | tf_op jit(solution)/shard_map/concatenate | solution.py:43
  75.3 10.3 %fusion.50 = f32[8,32,8192]{2,0,1:T(8,128)} fusion(bf16[8,47,8192]{2,0,1:T(8,128)(2,1)S(1)} %bitcast.109, f32[16,1,8192]{2,1,0:T(1,128)S(1)} %tile.9), kind=kOutput, calls=%fused_computation.83 | convolution fusion | flops 402653184 | bytes 15073280 | tf_op jit(solution)/shard_map/conv_general_dilated | solution.py:46
  85.6 14.2 %reshape.351 = f32[8,32,2,64,64]{4,3,2,0,1:T(8,128)} reshape(f32[8,32,8192]{2,0,1:T(8,128)} %fusion.50) | data formatting | bytes 16777216 | tf_op jit(solution)/shard_map/reshape | solution.py:55
  99.8 33.7 %fusion.5 = f32[8,32,64,2,64]{4,2,3,1,0:T(8,128)} fusion(f32[1,64,2,64]{3,1,0,2:T(8,128)S(1)} %get-tuple-element.16, f32[1,64,2,64]{3,1,0,2:T(8,128)S(1)} %get-tuple-element.15, f32[8,32,2,64,64]{4,3,2,0,1:T(8,128)} %reshape.351), kind=kOutput, calls=%fused_computation.6 | convolution fusion | flops 3221241856 | bytes 16842752 | tf_op jit(solution)/shard_map/sfrab,rapk->sfbpk/dot_general | solution.py:57
  133.5 7.2 %multiply_add_fusion = (f32[8,32,64,1,64]{4,2,3,1,0:T(8,128)S(1)}, f32[8,32,64,1,64]{4,2,3,1,0:T(8,128)S(1)}) fusion(f32[8,32,64,2,64]{4,2,3,1,0:T(8,128)} %fusion.5, f32[64,64]{1,0:T(8,128)S(1)} %get-tuple-element.21, f32[64,64]{1,0:T(8,128)S(1)} %get-tuple-element.22), kind=kLoop, calls=%fused_computation.9 | loop fusion | flops 6291456 | bytes 16809984 | tf_op jit(solution)/shard_map/add | solution.py:64
  140.7 12.6 %fusion.8 = bf16[8,32,2,32,64]{4,3,1,0,2:T(8,128)(2,1)} fusion(f32[8,32,64,1,64]{4,2,3,1,0:T(8,128)S(1)} %get-tuple-element.6, f32[8,32,64,1,64]{4,2,3,1,0:T(8,128)S(1)} %get-tuple-element.5, f32[1,64,2,32]{1,3,0,2:T(8,128)S(1)} %get-tuple-element.18, f32[1,64,2,32]{1,3,0,2:T(8,128)S(1)} %get-tuple-element.17), kind=kOutput, calls=%fused_computation.11 | convolution fusion | flops 1613766656 | bytes 10518528 | tf_op jit(solution)/shard_map/sfbpk,pbqj->sfqjk/dot_general | solution.py:69
  153.4 22.4 %copy.84 = bf16[8,32,2,32,64]{1,2,0,4,3:T(2,128)(2,1)} copy(bf16[8,32,2,32,64]{4,3,1,0,2:T(8,128)(2,1)} %fusion.8) | data formatting | bytes 4194304 | tf_op jit(solution)/shard_map/convert_element_type | solution.py:72
  175.7 10.1 %reshape.366 = bf16[8,2,65536]{2,1,0:T(2,128)(2,1)S(1)} reshape(bf16[2048,8,2,32]{3,2,1,0:T(2,128)(2,1)} %bitcast.104) | data formatting | bytes 4194304
  185.9 33.2 %all_to_all.18 = bf16[8,2,65536]{2,1,0:T(2,128)(2,1)} all-to-all(bf16[8,2,65536]{2,1,0:T(2,128)(2,1)S(1)} %reshape.366), channel_id=1, replica_groups=mesh['stn'=32,'tm'=8] {'tm'}, dimensions={0} | all-to-all | bytes 4194304 | tf_op jit(solution)/shard_map/all_to_all | solution.py:98
  219.0 8.7 %reshape.367 = bf16[2048,8,2,32]{3,2,1,0:T(2,128)(2,1)} reshape(bf16[8,2,65536]{2,1,0:T(2,128)(2,1)} %all_to_all.18) | data formatting | bytes 4194304
  227.7 17.8 %copy.86 = bf16[8,32,2,8,256]{4,1,3,2,0:T(8,128)(2,1)S(1)} copy(bf16[8,32,2,8,256]{1,2,0,4,3:T(2,128)(2,1)} %bitcast.105) | data formatting | bytes 4194304 | tf_op jit(solution)/shard_map/all_to_all | solution.py:98
  248.7 7.2 %collective-permute-start.1 = (bf16[8,256,2,256]{1,0,2,3:T(8,128)(2,1)}, bf16[8,256,2,256]{1,0,2,3:T(8,128)(2,1)}, u32[]{:S(2)}, u32[]{:S(2)}) collective-permute-start(bf16[8,256,2,256]{1,0,2,3:T(8,128)(2,1)} %copy.59), channel_id=1, source_target_pairs={{248,0},{0,8},{8,16},{16,24},{24,32},{32,40},{40,48},{48,56},{56,6... | collective-permute-start | bytes 6291464 | tf_op jit(solution)/shard_map/ppermute | solution.py:17
  255.9 23.3 %collective-permute-done.1 = bf16[8,256,2,256]{1,0,2,3:T(8,128)(2,1)} collective-permute-done((bf16[8,256,2,256]{1,0,2,3:T(8,128)(2,1)}, bf16[8,256,2,256]{1,0,2,3:T(8,128)(2,1)}, u32[]{:S(2)}, u32[]{:S(2)}) %collective-permute-start.1) | collective-permute-done | bytes 2097184 | tf_op jit(solution)/shard_map/ppermute | solution.py:17
  279.2 4.6 %collective-permute-start.2 = (bf16[8,256,2,256]{1,0,2,3:T(8,128)(2,1)}, bf16[8,256,2,256]{1,0,2,3:T(8,128)(2,1)}, u32[]{:S(2)}, u32[]{:S(2)}) collective-permute-start(bf16[8,256,2,256]{1,0,2,3:T(8,128)(2,1)} %collective-permute-done.1), channel_id=1, source_target_pairs={{248,0},{0,8},{8,16},{16,24},{24,32},{32,40},{40,48},{48,56},{56,6... | collective-permute-start | bytes 6291464 | tf_op jit(solution)/shard_map/ppermute | solution.py:17
  287.2 4.6 %copy.74 = bf16[8,256,2,256,1]{1,0,4,2,3:T(8,128)(2,1)} copy(bf16[8,256,2,256,1]{3,1,2,0,4:T(8,128)(2,1)} %bitcast.108) | data formatting | bytes 4194304 | tf_op jit(solution)/shard_map/all_to_all | solution.py:98
  291.8 15.3 %collective-permute-done.2 = bf16[8,256,2,256]{1,0,2,3:T(8,128)(2,1)} collective-permute-done((bf16[8,256,2,256]{1,0,2,3:T(8,128)(2,1)}, bf16[8,256,2,256]{1,0,2,3:T(8,128)(2,1)}, u32[]{:S(2)}, u32[]{:S(2)}) %collective-permute-start.2) | collective-permute-done | bytes 2097184 | tf_op jit(solution)/shard_map/ppermute | solution.py:17
  307.1 4.7 %collective-permute-start.3 = (bf16[8,256,2,256]{1,0,2,3:T(8,128)(2,1)}, bf16[8,256,2,256]{1,0,2,3:T(8,128)(2,1)}, u32[]{:S(2)}, u32[]{:S(2)}) collective-permute-start(bf16[8,256,2,256]{1,0,2,3:T(8,128)(2,1)} %collective-permute-done.2), channel_id=1, source_target_pairs={{248,0},{0,8},{8,16},{16,24},{24,32},{32,40},{40,48},{48,56},{56,6... | collective-permute-start | bytes 6291464 | tf_op jit(solution)/shard_map/ppermute | solution.py:17
  311.8 6.3 %convolution_bitcast_fusion.3 = f32[2,8,2,8,256]{3,1,0,2,4:T(8,128)S(1)} fusion(bf16[8,256,2,256,1]{1,0,4,2,3:T(8,128)(2,1)} %copy.74, bf16[8,256,2,256,1]{1,0,2,4,3:T(8,128)(2,1)S(1)} %copy.75), kind=kOutput, calls=%fused_computation.15 | convolution fusion | flops 33554432 | bytes 4456448 | tf_op jit(solution)/shard_map/sfrc,tfqc->rsqtc/dot_general | solution.py:76
  321.2 6.3 %convolution_bitcast_fusion.2 = f32[2,8,2,8,256]{3,1,0,2,4:T(8,128)S(1)} fusion(bf16[8,256,2,256,1]{1,0,2,4,3:T(8,128)(2,1)S(1)} %copy.75, bf16[8,256,2,256]{1,0,2,3:T(8,128)(2,1)} %collective-permute-done.1), kind=kOutput, calls=%fused_computation.14 | convolution fusion | flops 33554432 | bytes 4456448 | tf_op jit(solution)/shard_map/sfrc,tfqc->rsqtc/dot_general | solution.py:76
  330.6 6.3 %convolution_bitcast_fusion.1 = f32[2,8,2,8,256]{3,1,0,2,4:T(8,128)S(1)} fusion(bf16[8,256,2,256,1]{1,0,2,4,3:T(8,128)(2,1)S(1)} %copy.75, bf16[8,256,2,256]{1,0,2,3:T(8,128)(2,1)} %collective-permute-done.2), kind=kOutput, calls=%fused_computation.13 | convolution fusion | flops 33554432 | bytes 4456448 | tf_op jit(solution)/shard_map/sfrc,tfqc->rsqtc/dot_general | solution.py:76
  340.0 6.3 %convolution_bitcast_fusion = f32[2,8,2,8,256]{3,1,0,2,4:T(8,128)S(1)} fusion(bf16[8,256,2,256,1]{1,0,2,4,3:T(8,128)(2,1)S(1)} %copy.75, bf16[8,256,2,256]{1,0,2,3:T(8,128)(2,1)} %collective-permute-done.3), kind=kOutput, calls=%fused_computation.12 | convolution fusion | flops 33554432 | bytes 4456448 | tf_op jit(solution)/shard_map/sfrc,tfqc->rsqtc/dot_general | solution.py:76
  (28 shorter events, 23.6 us)
Async XLA Ops:
  5.3 45.0 %collective-permute-start = (bf16[8,15,2,4096]{3,2,1,0:T(2,128)(2,1)}, bf16[8,15,2,4096]{3,2,1,0:T(2,128)(2,1)S(1)}, u32[]{:S(2)}, u32[]{:S(2)}) collective-permute-start(bf16[8,15,2,4096]{3,2,1,0:T(2,128)(2,1)} %slice.57), channel_id=1, source_target_pairs={{0,1},{1,2},{2,3},{3,4},{4,5},{5,6},{6,7},{8,9},{9,10},{10,11},{11... | collective-permute-start | bytes 5898248 | tf_op jit(solution)/shard_map/ppermute | solution.py:23
  245.5 38.3 %copy-start = (bf16[8,32,2,8,256]{4,1,3,2,0:T(8,128)(2,1)}, bf16[8,32,2,8,256]{4,1,3,2,0:T(8,128)(2,1)S(1)}, u32[]{:S(2)}) copy-start(bf16[8,32,2,8,256]{4,1,3,2,0:T(8,128)(2,1)S(1)} %copy.86) | copy-start | bytes 6291460
  248.7 30.5 %collective-permute-start.1 = (bf16[8,256,2,256]{1,0,2,3:T(8,128)(2,1)}, bf16[8,256,2,256]{1,0,2,3:T(8,128)(2,1)}, u32[]{:S(2)}, u32[]{:S(2)}) collective-permute-start(bf16[8,256,2,256]{1,0,2,3:T(8,128)(2,1)} %copy.59), channel_id=1, source_target_pairs={{248,0},{0,8},{8,16},{16,24},{24,32},{32,40},{40,48},{48,56},{56,6... | collective-permute-start | bytes 6291464 | tf_op jit(solution)/shard_map/ppermute | solution.py:17
  279.2 27.9 %collective-permute-start.2 = (bf16[8,256,2,256]{1,0,2,3:T(8,128)(2,1)}, bf16[8,256,2,256]{1,0,2,3:T(8,128)(2,1)}, u32[]{:S(2)}, u32[]{:S(2)}) collective-permute-start(bf16[8,256,2,256]{1,0,2,3:T(8,128)(2,1)} %collective-permute-done.1), channel_id=1, source_target_pairs={{248,0},{0,8},{8,16},{16,24},{24,32},{32,40},{40,48},{48,56},{56,6... | collective-permute-start | bytes 6291464 | tf_op jit(solution)/shard_map/ppermute | solution.py:17
  307.1 32.9 %collective-permute-start.3 = (bf16[8,256,2,256]{1,0,2,3:T(8,128)(2,1)}, bf16[8,256,2,256]{1,0,2,3:T(8,128)(2,1)}, u32[]{:S(2)}, u32[]{:S(2)}) collective-permute-start(bf16[8,256,2,256]{1,0,2,3:T(8,128)(2,1)} %collective-permute-done.2), channel_id=1, source_target_pairs={{248,0},{0,8},{8,16},{16,24},{24,32},{32,40},{40,48},{48,56},{56,6... | collective-permute-start | bytes 6291464 | tf_op jit(solution)/shard_map/ppermute | solution.py:17
where the time goes:
time: 354 us; the launch traced here: 348 us
  local copies, waits for them, and re-layouts  105 us (30%)
  matrix products  81.8 us (23%)
  waiting for transfers between devices  77.6 us (22%)
  blocking collectives  33.2 us (9%)
  other arithmetic  30.6 us (9%)
  starting transfers between devices  19.9 us (6%)
    ppermute x1, waiting for transfers between devices, passed_along_2(): return lax.ppermute(shard, axis, pairs)  39 us
    ppermute x3, waiting for transfers between devices, passed_along(): return lax.ppermute(block, axis, route)  38.6 us
    dot_general x1, matrix products, channelise(): jnp.einsum('sfrab,rapk->sfbpk', grid_form, real_form(cos_one, sin_one), p...  33.7 us
    all_to_all x1, blocking collectives, local(): lax.all_to_all(spectrum, 'tm', split_axis=3, concat_axis=1, tiled=True)  33.2 us
    all_to_all x4, local copies, waits for them, and re-layouts, local(): lax.all_to_all(spectrum, 'tm', split_axis=3, concat_axis=1, tiled=True)  28.9 us
    dot_general x4, matrix products, correlate(): jnp.einsum('sfrc,tfqc->rsqtc', own_block, other_block, preferred_element_...  25.2 us
    convert_element_type x1, local copies, waits for them, and re-layouts, channelise(): spectrum.reshape(signals, count_frames, 2, CHANS).astype(jnp.bfloat16)  22.4 us
    unnamed x4, local copies, waits for them, and re-layouts  18.8 us
  transfers between devices with their start and end apart: 4, of which 3 were waited for; matrix products, arithmetic and copies ran while one was open for 11% of the time, Pallas kernels for 0%

commit v1 on v0

v1 whole, which is shorter than its diff:
```python
import functools
import math

import jax
import jax.numpy as jnp
import numpy as np
from jax import lax
from jax.experimental import pallas as pl
from jax.experimental.pallas import tpu as pltpu
from jax.sharding import PartitionSpec as P

MESH = pl.DeviceIdType.MESH
TAPS = 16
SIG = 8
FR = 32
EXT = 48
QUAD = 4
TMS = 8
PLANE = QUAD * TMS
NT = (((1,), (1,)), ((), ()))


def split(table):
    high = table.astype(jnp.bfloat16)
    low = (table - high.astype(np.float64)).astype(jnp.bfloat16)
    return high, low


def tables():
    hi = np.arange(32)
    lo = np.arange(128)
    c1 = np.arange(32)
    c2 = np.arange(64)
    angle = 2.0 * math.pi * (np.outer(c1, hi) % 32) / 32.0
    first = np.zeros((2, 32, 32, 2))
    first[0, :, :, 0] = np.cos(angle)
    first[0, :, :, 1] = np.sin(angle)
    first[1, :, :, 0] = -np.sin(angle)
    first[1, :, :, 1] = np.cos(angle)
    high, low = split(first.reshape(64, 64))
    w1 = np.concatenate([high, low, high], axis=1)
    angle = 2.0 * math.pi * np.outer(c1, lo) / 4096.0
    turn = np.stack([np.cos(angle), np.sin(angle)]).astype(np.float32)
    angle = 2.0 * math.pi * (np.outer(c2, lo) % 128) / 128.0
    second = np.zeros((64, 2, 2, 128))
    second[:, 0, 0] = np.cos(angle)
    second[:, 0, 1] = np.sin(angle)
    second[:, 1, 0] = -np.sin(angle)
    second[:, 1, 1] = np.cos(angle)
    high, low = split(second.reshape(128, 256) / 64.0)
    w2 = np.concatenate([high, low], axis=0)
    return w1, turn, w2


def kernel(
    v_hbm, taps_ref, w1_ref, turn_ref, w2_ref, out_ref,
    vbuf, vf, yf, zh, zl, msg, recv, mrg, zrecv, qf, psend, obuf,
    v_sem, send_sem, recv_sem, zsend_sem, zrecv_sem, rsend_sem, rrecv_sem,
):
    stn = lax.axis_index("stn")
    tm = lax.axis_index("tm")
    z = stn // QUAD
    q_me = stn % QUAD
    me = tm * QUAD + q_me
    up = ((z + 1) % 8) * QUAD + q_me
    down = ((z + 7) % 8) * QUAD + q_me

    def place(plane_index):
        return (z * QUAD + plane_index % QUAD, plane_index // QUAD)

    def load(s):
        return pltpu.make_async_copy(v_hbm.at[s], vbuf.at[s], v_sem.at[s])

    for s in range(SIG):
        load(s).start()

    barrier = pltpu.get_barrier_semaphore()

    def greet(j, carry):
        pl.semaphore_signal(barrier, inc=1, device_id=place((me + j) % PLANE), device_id_type=MESH)
        return carry

    lax.fori_loop(1, PLANE, greet, 0)
    pl.semaphore_signal(barrier, inc=1, device_id=(up, tm), device_id_type=MESH)
    pl.semaphore_signal(barrier, inc=1, device_id=(down, tm), device_id_type=MESH)

    def channelise(s):
        load(s).wait()

        def widen(f, carry):
            vf[f] = vbuf[s, f].astype(jnp.float32)
            return carry

        lax.fori_loop(0, FR, widen, 0)

        def fir(g, carry):
            rows = pl.ds(pl.multiple_of(g * 8, 8), 8)
            taps = [taps_ref[m, rows, :] for m in range(TAPS)]
            frames = {}
            for f_out in range(FR + TAPS - 1):
                if f_out < FR:
                    frames[f_out] = vf[f_out, rows, :]
                total = None
                for m in range(TAPS):
                    f_in = f_out - (TAPS - 1) + m
                    if 0 <= f_in < FR:
                        term = taps[m] * frames[f_in]
                        total = term if total is None else total + term
                yf[f_out, rows, :] = total
            return carry

        lax.fori_loop(0, 8, fir, 0)

        def first_stage(pair, carry):
            x = jnp.concatenate([yf[2 * pair], yf[2 * pair + 1]], axis=1)
            high = x.astype(jnp.bfloat16)
            low = (x - high.astype(jnp.float32)).astype(jnp.bfloat16)
            y = jnp.dot(
                w1_ref[...], jnp.concatenate([high, high, low], axis=0),
                preferred_element_type=jnp.float32,
            )
            parts = []
            for j in range(2):
                yr = y[0:32, 128 * j:128 * j + 128]
                yi = y[32:64, 128 * j:128 * j + 128]
                zr = yr * turn_ref[0] + yi * turn_ref[1]
                zi = yi * turn_ref[0] - yr * turn_ref[1]
                parts.append((zr, zi))
            rows = pl.ds(pl.multiple_of(pair * 16, 16), 16)
            for q in range(QUAD):
                for r in range(2):
                    block = jnp.concatenate([parts[0][r][8 * q:8 * q + 8], parts[1][r][8 * q:8 * q + 8]], axis=0)
                    high = block.astype(jnp.bfloat16)
                    zh[q, rows, 128 * r:128 * r + 128] = high
                    zl[q, rows, 128 * r:128 * r + 128] = (block - high.astype(jnp.float32)).astype(jnp.bfloat16)
            return carry

        lax.fori_loop(0, EXT // 2, first_stage, 0)

        for q in range(QUAD):
            full = lax.dot_general(w2_ref[...], zh[q], NT, preferred_element_type=jnp.float32)
            rest = lax.dot_general(w2_ref[0:128, :], zl[q], NT, preferred_element_type=jnp.float32)
            spectra = (full[0:128] + full[128:256] + rest).astype(jnp.bfloat16)
            for t in range(TMS):
                msg[s, t * QUAD + q] = spectra[16 * t:16 * t + 16]

    def send(s):
        def one(j, carry):
            to = (me + j) % PLANE
            pltpu.make_async_remote_copy(
                src_ref=msg.at[s, to], dst_ref=recv.at[s, me],
                send_sem=send_sem.at[s], recv_sem=recv_sem.at[s],
                device_id=place(to), device_id_type=MESH,
            ).start()
            return carry

        pltpu.make_async_copy(msg.at[s, me], recv.at[s, me], recv_sem.at[s]).start()
        lax.fori_loop(1, PLANE, one, 0)

    def pass_up(s):
        return pltpu.make_async_remote_copy(
            src_ref=mrg.at[s, pl.ds(1, 3)], dst_ref=zrecv.at[s],
            send_sem=zsend_sem.at[s], recv_sem=zrecv_sem.at[s],
            device_id=(up, tm), device_id_type=MESH,
        )

    def spread(values, slot, s, tile):
        wide = values.astype(jnp.float32)
        for g in range(2):
            qf[tile, pl.ds(g * 512 + slot * 8 + s, 8, stride=64), :] = wide[8 * g:8 * g + 8]

    def merge(s):
        pltpu.make_async_copy(recv.at[s], recv.at[s], recv_sem.at[s]).wait()
        for q in range(QUAD):
            for t in range(TMS):
                early = recv[s, t * QUAD + q, :, 0:128]
                if t > 0:
                    before = recv[s, (t - 1) * QUAD + q, :, 256:384]
                    early = (early.astype(jnp.float32) + before.astype(jnp.float32)).astype(jnp.bfloat16)
                late = recv[s, t * QUAD + q, :, 128:256]
                mrg[s, q, t, :, 0:128] = early
                mrg[s, q, t, :, 128:256] = late
                spread(early, 3 - q, s, 2 * t)
                spread(late, 3 - q, s, 2 * t + 1)
        pass_up(s).start()

    def merge_passed(s, carry):
        pass_up(s).wait_recv()
        for k in range(3):
            for t in range(TMS):
                for h in range(2):
                    spread(zrecv[s, k, t, :, 128 * h:128 * h + 128], 6 - k, s, 2 * t + h)
        return carry

    yf[EXT - 1] = jnp.zeros((64, 128), jnp.float32)

    def clear(i, carry):
        qf[:, pl.ds(pl.multiple_of(i * 64 + 56, 8), 8), :] = jnp.zeros((16, 8, 128), jnp.float32)
        return carry

    lax.fori_loop(0, 16, clear, 0)

    channelise(0)
    pl.semaphore_wait(barrier, PLANE + 1)
    send(0)

    def step(s, carry):
        @pl.when(s < SIG)
        def _():
            channelise(s)
            send(s)

        @pl.when(s >= 2)
        def _():
            merge(s - 2)

        return carry

    lax.fori_loop(1, SIG + 2, step, 0)
    lax.fori_loop(0, SIG, merge_passed, 0)

    lane = lax.broadcasted_iota(jnp.int32, (1, 2048), 1) % 8
    lane_out = lax.broadcasted_iota(jnp.int32, (1, 128), 1)
    sign = jnp.where(lane_out < 64, 1.0, -1.0).astype(jnp.float32)
    first_half = (lane_out // 32) % 2 == 0

    def gram(c2):
        rows = pl.ds(pl.multiple_of(c2 * 128, 128), 128)
        b = jnp.concatenate([qf[k, rows, :].astype(jnp.bfloat16) for k in range(16)], axis=1)
        a = jnp.concatenate([b[0:32], b[64:96]], axis=0)
        stacked = jnp.concatenate(
            [jnp.where(lane == c1, a, jnp.zeros_like(a)) for c1 in range(8)], axis=0
        )
        out = lax.dot_general(stacked, b, NT, preferred_element_type=jnp.float32)
        return out * (1.0 / 256.0)

    def result(c2lo, i):
        return pltpu.make_async_remote_copy(
            src_ref=psend.at[c2lo, 3 - i], dst_ref=obuf.at[c2lo, q_me],
            send_sem=rsend_sem.at[c2lo], recv_sem=rrecv_sem.at[c2lo],
            device_id=(z * QUAD + i, tm), device_id_type=MESH,
        )

    def correlate(c2lo, carry):
        grams = [gram(c2lo), gram(c2lo + 4)]
        for c1 in range(8):
            packed = []
            for full in grams:
                g0 = full[64 * c1:64 * c1 + 32]
                g1 = full[64 * c1 + 32:64 * c1 + 64]
                packed.append(pltpu.roll(g1, 64, 1) + sign * g0)
            for slot in range(QUAD):
                low = packed[0][8 * slot:8 * slot + 8]
                high = packed[1][8 * slot:8 * slot + 8]
                if slot:
                    low = pltpu.roll(low, 128 - 8 * slot, 1)
                high = pltpu.roll(high, (128 - 8 * slot + 32) % 128, 1)
                psend[c2lo, slot, c1] = jnp.where(first_half, low, high)
        pltpu.make_async_copy(psend.at[c2lo, 3 - q_me], obuf.at[c2lo, q_me], rrecv_sem.at[c2lo]).start()
        for j in range(1, QUAD):
            result(c2lo, (q_me + j) % QUAD).start()
        return carry

    lax.fori_loop(0, 4, correlate, 0)

    for c2lo in range(4):
        pltpu.make_async_copy(obuf.at[c2lo], obuf.at[c2lo], rrecv_sem.at[c2lo]).wait()

    flat = obuf.reshape(4 * QUAD * 8 * SIG, 128)
    for s in range(SIG):
        block = flat[pl.ds(s, 128, stride=8), :].T
        for part in range(2):
            for half in range(2):
                at = (part * 2 + half) * 32
                out_ref[part, s, :, 128 * half:128 * half + 128] = block[at:at + 32]

    def settle(s, carry):
        pltpu.make_async_copy(msg.at[s, pl.ds(0, PLANE - 1)], recv.at[s, pl.ds(0, PLANE - 1)], send_sem.at[s]).wait()
        pass_up(s).wait_send()
        return carry

    lax.fori_loop(0, SIG, settle, 0)
    for c2lo in range(4):
        pltpu.make_async_copy(
            psend.at[c2lo, pl.ds(0, 3)], obuf.at[c2lo, pl.ds(0, 3)], rsend_sem.at[c2lo]
        ).wait()


def local(voltage, fir_taps):
    rows = voltage.reshape(SIG, FR, 2, 32, 128).transpose(0, 1, 3, 2, 4).reshape(SIG, FR, 64, 128)
    taps = jnp.broadcast_to(fir_taps.reshape(TAPS, 32, 1, 128), (TAPS, 32, 2, 128)).reshape(TAPS, 64, 128)
    w1, turn, w2 = tables()
    vmem = pl.BlockSpec(memory_space=pltpu.VMEM)
    return pl.pallas_call(
        kernel,
        out_shape=jax.ShapeDtypeStruct((2, SIG, 32, 256), jnp.float32),
        in_specs=[pl.BlockSpec(memory_space=pl.ANY), vmem, vmem, vmem, vmem],
        out_specs=vmem,
        scratch_shapes=[
            pltpu.VMEM((SIG, FR, 64, 128), jnp.bfloat16),
            pltpu.VMEM((FR, 64, 128), jnp.float32),
            pltpu.VMEM((EXT, 64, 128), jnp.float32),
            pltpu.VMEM((QUAD, EXT * 8, 256), jnp.bfloat16),
            pltpu.VMEM((QUAD, EXT * 8, 256), jnp.bfloat16),
            pltpu.VMEM((SIG, PLANE, 16, 384), jnp.bfloat16),
            pltpu.VMEM((SIG, PLANE, 16, 384), jnp.bfloat16),
            pltpu.VMEM((SIG, QUAD, TMS, 16, 256), jnp.bfloat16),
            pltpu.VMEM((SIG, 3, TMS, 16, 256), jnp.bfloat16),
            pltpu.VMEM((16, 16 * 64, 128), jnp.float32),
            pltpu.VMEM((4, QUAD, 8, SIG, 128), jnp.float32),
            pltpu.VMEM((4, QUAD, 8, SIG, 128), jnp.float32),
            pltpu.SemaphoreType.DMA((SIG,)),
            pltpu.SemaphoreType.DMA((SIG,)),
            pltpu.SemaphoreType.DMA((SIG,)),
            pltpu.SemaphoreType.DMA((SIG,)),
            pltpu.SemaphoreType.DMA((SIG,)),
            pltpu.SemaphoreType.DMA((4,)),
            pltpu.SemaphoreType.DMA((4,)),
        ],
        compiler_params=pltpu.CompilerParams(
            collective_id=0, has_side_effects=True, vmem_limit_bytes=60 * 1024 * 1024
        ),
    )(rows, taps, jnp.asarray(w1), jnp.asarray(turn), jnp.asarray(w2))


def solution(mesh):
    return jax.shard_map(
        local,
        mesh=mesh,
        in_specs=(P("stn", "tm", None, None), P()),
        out_specs=P(None, "stn", None, "tm"),
        check_vma=False,
    )
```

time: 354 us -> 92.6 us (0.26)
  the two profiles are of different devices: /device:TPU:99 before, /device:TPU:1 now
where the time goes in v1:
time: 92.6 us; the launch traced here: 92.4 us
  Pallas kernels  88.5 us (96%)
  local copies, waits for them, and re-layouts  3.86 us (4%)
    pallas_call x1, Pallas kernels, local(): pl.pallas_call(kernel, out_shape=jax.ShapeDtypeStruct((2, SIG, 32, 256),...  88.5 us
    unnamed x2, local copies, waits for them, and re-layouts  2.88 us

profile of v1, /device:TPU:1, one launch (start us, length us, event | category | flops | bytes accessed | tf_op | source)
XLA Modules:
  0.0 92.4 jit_solution(10913823012881519381)
XLA Ops:
  0.0 1.0 %copy.7 = f32[2,8,32,128]{3,2,1,0:T(8,128)S(1)} copy(f32[2,8,32,128]{3,1,2,0:T(8,128)} %bitcast.11) | data formatting | bytes 524288
  1.0 1.0 %broadcast_in_dim.8 = f32[16,32,2,128]{3,2,1,0:T(2,128)} broadcast(f32[16,32,128]{2,1,0:T(8,128)S(1)} %bitcast.10), dimensions={0,1,3} | broadcast | bytes 786432 | tf_op jit(solution)/shard_map/broadcast_in_dim | solution.py:291
  2.0 88.5 %shard_map.55 = f32[2,8,32,256]{3,2,1,0:T(8,128)} custom-call(bf16[8,32,64,128]{3,2,1,0:T(8,128)(2,1)} %bitcast.8, f32[16,64,128]{2,1,0:T(8,128)} %bitcast.9, bf16[64,192]{1,0:T(8,128)(2,1)} %constant.6.clone.w1_ref, f32[2,32,128]{2,1,0:T(8,128)} %constant.7.clone.turn_ref, bf16[256,256]{1,0:T(8,128)(2,1)} %constant.8.clone.w2_ref), custom_call_target="tpu_custom_call" | custom-call | tf_op jit(solution)/shard_map/pallas_call | solution.py:294
  90.5 1.9 %copy.9 = f32[2,8,32,256]{3,2,1,0:T(8,128)} copy(f32[2,8,32,256]{3,2,1,0:T(8,128)} %shard_map.55) | data formatting | bytes 1048576

commit v2 on v1

--- a/solution.py
+++ b/solution.py
@@ -17,6 +17,7 @@
 QUAD = 4
 TMS = 8
 PLANE = QUAD * TMS
+GROUP = 16
 NT = (((1,), (1,)), ((), ()))
 
 
@@ -53,8 +54,8 @@
 
 
 def kernel(
-    v_hbm, taps_ref, w1_ref, turn_ref, w2_ref, out_ref,
-    vbuf, vf, yf, zh, zl, msg, recv, mrg, zrecv, qf, psend, obuf,
+    v_hbm, fir_ref, w1_ref, turn_ref, w2_ref, out_ref,
+    taps_ref, vbuf, vf, yf, zh, zl, msg, recv, mrg, zrecv, qf, psend, obuf,
     v_sem, send_sem, recv_sem, zsend_sem, zrecv_sem, rsend_sem, rrecv_sem,
 ):
     stn = lax.axis_index("stn")
@@ -95,7 +96,7 @@
 
         def fir(g, carry):
             rows = pl.ds(pl.multiple_of(g * 8, 8), 8)
-            taps = [taps_ref[m, rows, :] for m in range(TAPS)]
+            taps = [taps_ref[pl.ds(pl.multiple_of(g * 8 + m * 64, 8), 8), :] for m in range(TAPS)]
             frames = {}
             for f_out in range(FR + TAPS - 1):
                 if f_out < FR:
@@ -111,8 +112,8 @@
 
         lax.fori_loop(0, 8, fir, 0)
 
-        def first_stage(pair, carry):
-            x = jnp.concatenate([yf[2 * pair], yf[2 * pair + 1]], axis=1)
+        def first_stage(step, carry):
+            x = jnp.concatenate([yf[step * GROUP + j] for j in range(GROUP)], axis=1)
             high = x.astype(jnp.bfloat16)
             low = (x - high.astype(jnp.float32)).astype(jnp.bfloat16)
             y = jnp.dot(
@@ -120,22 +121,22 @@
                 preferred_element_type=jnp.float32,
             )
             parts = []
-            for j in range(2):
+            for j in range(GROUP):
                 yr = y[0:32, 128 * j:128 * j + 128]
                 yi = y[32:64, 128 * j:128 * j + 128]
                 zr = yr * turn_ref[0] + yi * turn_ref[1]
                 zi = yi * turn_ref[0] - yr * turn_ref[1]
                 parts.append((zr, zi))
-            rows = pl.ds(pl.multiple_of(pair * 16, 16), 16)
+            rows = pl.ds(pl.multiple_of(step * (8 * GROUP), 8 * GROUP), 8 * GROUP)
             for q in range(QUAD):
                 for r in range(2):
-                    block = jnp.concatenate([parts[0][r][8 * q:8 * q + 8], parts[1][r][8 * q:8 * q + 8]], axis=0)
+                    block = jnp.concatenate([part[r][8 * q:8 * q + 8] for part in parts], axis=0)
                     high = block.astype(jnp.bfloat16)
                     zh[q, rows, 128 * r:128 * r + 128] = high
                     zl[q, rows, 128 * r:128 * r + 128] = (block - high.astype(jnp.float32)).astype(jnp.bfloat16)
             return carry
 
-        lax.fori_loop(0, EXT // 2, first_stage, 0)
+        lax.fori_loop(0, EXT // GROUP, first_stage, 0)
 
         for q in range(QUAD):
             full = lax.dot_general(w2_ref[...], zh[q], NT, preferred_element_type=jnp.float32)
@@ -159,38 +160,60 @@
 
     def pass_up(s):
         return pltpu.make_async_remote_copy(
-            src_ref=mrg.at[s, pl.ds(1, 3)], dst_ref=zrecv.at[s],
+            src_ref=mrg.at[s], dst_ref=zrecv.at[s],
             send_sem=zsend_sem.at[s], recv_sem=zrecv_sem.at[s],
             device_id=(up, tm), device_id_type=MESH,
         )
 
-    def spread(values, slot, s, tile):
-        wide = values.astype(jnp.float32)
+    def spread(wide, slot, s, tile):
         for g in range(2):
             qf[tile, pl.ds(g * 512 + slot * 8 + s, 8, stride=64), :] = wide[8 * g:8 * g + 8]
+
+    lane_of = lax.broadcasted_iota(jnp.int32, (1, 128), 1)
+
+    def exchange(tiles, bit, distance):
+        clear = (lane_of // distance) % 2 == 0
+        out = list(tiles)
+        for k in range(8):
+            if (k // bit) % 2 == 0:
+                a, b = tiles[k], tiles[k + bit]
+                out[k] = jnp.where(clear, a, pltpu.roll(b, distance, 1))
+                out[k + bit] = jnp.where(clear, pltpu.roll(a, 128 - distance, 1), b)
+        return out
 
     def merge(s):
         pltpu.make_async_copy(recv.at[s], recv.at[s], recv_sem.at[s]).wait()
         for q in range(QUAD):
-            for t in range(TMS):
-                early = recv[s, t * QUAD + q, :, 0:128]
-                if t > 0:
-                    before = recv[s, (t - 1) * QUAD + q, :, 256:384]
-                    early = (early.astype(jnp.float32) + before.astype(jnp.float32)).astype(jnp.bfloat16)
-                late = recv[s, t * QUAD + q, :, 128:256]
-                mrg[s, q, t, :, 0:128] = early
-                mrg[s, q, t, :, 128:256] = late
-                spread(early, 3 - q, s, 2 * t)
-                spread(late, 3 - q, s, 2 * t + 1)
+            for side in range(2):
+                tiles = []
+                for t in range(4 * side, 4 * side + 4):
+                    early = recv[s, t * QUAD + q, :, 0:128].astype(jnp.float32)
+                    if t > 0:
+                        before = recv[s, (t - 1) * QUAD + q, :, 256:384].astype(jnp.float32)
+                        early = (early + before).astype(jnp.bfloat16).astype(jnp.float32)
+                    tiles += [early, recv[s, t * QUAD + q, :, 128:256].astype(jnp.float32)]
+                tiles = exchange(tiles, 1, 4)
+                tiles = exchange(tiles, 2, 2)
+                tiles = exchange(tiles, 4, 1)
+                for k in range(8):
+                    c1 = (k % 2) * 4 + (k // 2 % 2) * 2 + k // 4
+                    spread(tiles[k], 3 - q, s, 2 * c1 + side)
+                    if q > 0:
+                        mrg[s, q - 1, 2 * c1 + side] = tiles[k].astype(jnp.bfloat16)
         pass_up(s).start()
 
     def merge_passed(s, carry):
         pass_up(s).wait_recv()
         for k in range(3):
-            for t in range(TMS):
-                for h in range(2):
-                    spread(zrecv[s, k, t, :, 128 * h:128 * h + 128], 6 - k, s, 2 * t + h)
-        return carry
+            for tile in range(16):
+                spread(zrecv[s, k, tile].astype(jnp.float32), 6 - k, s, tile)
+        return carry
+
+    for hi in range(32):
+        for g in range(2):
+            taps = fir_ref[8 * g:8 * g + 8, 128 * hi:128 * hi + 128]
+            for r in range(2):
+                taps_ref[pl.ds(512 * g + 2 * hi + r, 8, stride=64), :] = taps
 
     yf[EXT - 1] = jnp.zeros((64, 128), jnp.float32)
 
@@ -219,20 +242,15 @@
     lax.fori_loop(1, SIG + 2, step, 0)
     lax.fori_loop(0, SIG, merge_passed, 0)
 
-    lane = lax.broadcasted_iota(jnp.int32, (1, 2048), 1) % 8
-    lane_out = lax.broadcasted_iota(jnp.int32, (1, 128), 1)
-    sign = jnp.where(lane_out < 64, 1.0, -1.0).astype(jnp.float32)
-    first_half = (lane_out // 32) % 2 == 0
-
-    def gram(c2):
+    sign = jnp.where(lane_of < 64, 1.0, -1.0).astype(jnp.float32)
+    first_half = (lane_of // 32) % 2 == 0
+
+    def gram(c2, c1):
         rows = pl.ds(pl.multiple_of(c2 * 128, 128), 128)
-        b = jnp.concatenate([qf[k, rows, :].astype(jnp.bfloat16) for k in range(16)], axis=1)
+        b = jnp.concatenate([qf[2 * c1 + side, rows, :].astype(jnp.bfloat16) for side in range(2)], axis=1)
         a = jnp.concatenate([b[0:32], b[64:96]], axis=0)
-        stacked = jnp.concatenate(
-            [jnp.where(lane == c1, a, jnp.zeros_like(a)) for c1 in range(8)], axis=0
-        )
-        out = lax.dot_general(stacked, b, NT, preferred_element_type=jnp.float32)
-        return out * (1.0 / 256.0)
+        out = lax.dot_general(a, b, NT, preferred_element_type=jnp.float32) * (1.0 / 256.0)
+        return pltpu.roll(out[32:64], 64, 1) + sign * out[0:32]
 
     def result(c2lo, i):
         return pltpu.make_async_remote_copy(
@@ -242,13 +260,8 @@
         )
 
     def correlate(c2lo, carry):
-        grams = [gram(c2lo), gram(c2lo + 4)]
         for c1 in range(8):
-            packed = []
-            for full in grams:
-                g0 = full[64 * c1:64 * c1 + 32]
-                g1 = full[64 * c1 + 32:64 * c1 + 64]
-                packed.append(pltpu.roll(g1, 64, 1) + sign * g0)
+            packed = [gram(c2lo, c1), gram(c2lo + 4, c1)]
             for slot in range(QUAD):
                 low = packed[0][8 * slot:8 * slot + 8]
                 high = packed[1][8 * slot:8 * slot + 8]
@@ -288,7 +301,6 @@
 
 def local(voltage, fir_taps):
     rows = voltage.reshape(SIG, FR, 2, 32, 128).transpose(0, 1, 3, 2, 4).reshape(SIG, FR, 64, 128)
-    taps = jnp.broadcast_to(fir_taps.reshape(TAPS, 32, 1, 128), (TAPS, 32, 2, 128)).reshape(TAPS, 64, 128)
     w1, turn, w2 = tables()
     vmem = pl.BlockSpec(memory_space=pltpu.VMEM)
     return pl.pallas_call(
@@ -297,6 +309,7 @@
         in_specs=[pl.BlockSpec(memory_space=pl.ANY), vmem, vmem, vmem, vmem],
         out_specs=vmem,
         scratch_shapes=[
+            pltpu.VMEM((TAPS * 64, 128), jnp.float32),
             pltpu.VMEM((SIG, FR, 64, 128), jnp.bfloat16),
             pltpu.VMEM((FR, 64, 128), jnp.float32),
             pltpu.VMEM((EXT, 64, 128), jnp.float32),
@@ -304,8 +317,8 @@
             pltpu.VMEM((QUAD, EXT * 8, 256), jnp.bfloat16),
             pltpu.VMEM((SIG, PLANE, 16, 384), jnp.bfloat16),
             pltpu.VMEM((SIG, PLANE, 16, 384), jnp.bfloat16),
-            pltpu.VMEM((SIG, QUAD, TMS, 16, 256), jnp.bfloat16),
-            pltpu.VMEM((SIG, 3, TMS, 16, 256), jnp.bfloat16),
+            pltpu.VMEM((SIG, 3, 16, 16, 128), jnp.bfloat16),
+            pltpu.VMEM((SIG, 3, 16, 16, 128), jnp.bfloat16),
             pltpu.VMEM((16, 16 * 64, 128), jnp.float32),
             pltpu.VMEM((4, QUAD, 8, SIG, 128), jnp.float32),
             pltpu.VMEM((4, QUAD, 8, SIG, 128), jnp.float32),
@@ -320,7 +333,7 @@
         compiler_params=pltpu.CompilerParams(
             collective_id=0, has_side_effects=True, vmem_limit_bytes=60 * 1024 * 1024
         ),
-    )(rows, taps, jnp.asarray(w1), jnp.asarray(turn), jnp.asarray(w2))
+    )(rows, fir_taps, jnp.asarray(w1), jnp.asarray(turn), jnp.asarray(w2))
 
 
 def solution(mesh):

time: 92.6 us -> 70 us (0.76)
  Pallas kernels: 88.5 us -> 68 us
  local copies, waits for them, and re-layouts: 3.86 us -> 1.88 us
    pallas_call x1, Pallas kernels: 88.5 us -> 68 us  [local(): pl.pallas_call(kernel, out_shape=jax.ShapeDtypeStruct((2, SIG, 32, 256),...]
    unnamed x2 -> x1, local copies, waits for them, and re-layouts: 2.88 us -> 1.88 us
    broadcast_in_dim x1 -> x0, local copies, waits for them, and re-layouts: 0.98 us -> none  [local(): jnp.broadcast_to(fir_taps.reshape(TAPS, 32, 1, 128), (TAPS, 32, 2, 128))]
where the time goes in v2:
time: 70 us; the launch traced here: 69.9 us
  Pallas kernels  68 us (97%)
  local copies, waits for them, and re-layouts  1.88 us (3%)
    pallas_call x1, Pallas kernels, local(): pl.pallas_call(kernel, out_shape=jax.ShapeDtypeStruct((2, SIG, 32, 256),...  68 us
    unnamed x1, local copies, waits for them, and re-layouts  1.88 us

profile of v2, /device:TPU:1, one launch (start us, length us, event | category | flops | bytes accessed | tf_op | source)
XLA Modules:
  0.0 69.9 jit_solution(17011747462936147503)
XLA Ops:
  0.0 68.0 %shard_map.55 = f32[2,8,32,256]{3,2,1,0:T(8,128)} custom-call(bf16[8,32,64,128]{3,2,1,0:T(8,128)(2,1)} %bitcast.5, f32[16,4096]{1,0:T(8,128)} %fir_ref.1, bf16[64,192]{1,0:T(8,128)(2,1)} %constant.6.clone.w1_ref, f32[2,32,128]{2,1,0:T(8,128)} %constant.7.clone.turn_ref, bf16[256,256]{1,0:T(8,128)(2,1)} %constant.8.clone.w2_ref), custom_call_target="tpu_custom_call" | custom-call | tf_op jit(solution)/shard_map/pallas_call | solution.py:306
  68.0 1.9 %copy.8 = f32[2,8,32,256]{3,2,1,0:T(8,128)} copy(f32[2,8,32,256]{3,2,1,0:T(8,128)} %shard_map.55) | data formatting | bytes 1048576
